TPU v7x, 128 devices: a whole 4x4x4 slice. The times are simulated.
128 devices in a mesh: band: 8 (over y, x_lo), loc: 16 (over z, x_hi, core).
Axes of the slice: x: 4 (x_hi: 2, x_lo: 2; x = x_hi * 2 + x_lo), y: 4, z: 4, core: 2. Of those that a mesh axis runs over, the one named last changes fastest.
Arguments:
- tokens: bfloat16 [4096, 16, 768], P('loc', 'band'), may hold values from -6 to 6
- band_index: int32 [16], replicated, may hold values from 0 to 15, each once
- band_table: float32 [16, 768], replicated, may hold values from -3 to 3
- window_ids: int32 [4096], replicated, may hold values from 0 to 1, as said below
- spatial_qkv: bfloat16 [768, 2304], replicated
- spatial_out: bfloat16 [768, 768], replicated, may hold values from -0.21875 to 0.21875
- channel_qkv: bfloat16 [768, 2304], replicated
- channel_out: bfloat16 [768, 768], replicated, may hold values from -0.21875 to 0.21875
- up_weight: bfloat16 [768, 3072], replicated, may hold values from -0.21875 to 0.21875
- down_weight: bfloat16 [3072, 768], replicated, may hold values from -0.109375 to 0.109375
Outputs:
- joined: bfloat16 [4096, 16, 768], P('loc', 'band')
Inputs may be any that keep to these rules, and one draw needn't show every extreme that they name: `window_ids`: each of the 2 windows holds exactly 2048 locations, and each aligned block of 256 locations holds exactly 128 locations of each window. `band_index`: each of the 16 band numbers once.
All inputs are finite; a program needn't handle non-finite values.
Results may differ from a plain program's by a relative error of at most 0.014.
Values may be sent and summed in bfloat16 or wider, within the bound.
A program may use at most 128 MiB of HBM per device.

v0:
```python
import jax
import jax.numpy as jnp
from jax import lax
from jax.sharding import PartitionSpec as P

HEADS = 12
HEAD_DIM = 64


def norm_rows(values):
    centre = values - jnp.mean(values, axis=-1, keepdims=True)
    spread = jnp.mean(centre * centre, axis=-1, keepdims=True)
    return centre * lax.rsqrt(spread + 1e-05)


def attend(state, query, query_ids, keys, values, key_ids):
    scale = HEAD_DIM ** (-0.5)
    rows, band_dev, width = query.shape
    count = keys.shape[0]
    block = 512
    query_heads = query.reshape(rows, band_dev, HEADS, HEAD_DIM)

    def step(carry, index):
        first = index * block
        key_block = lax.dynamic_slice_in_dim(keys, first, block, 0).reshape(
            block, band_dev, HEADS, HEAD_DIM
        )
        value_block = lax.dynamic_slice_in_dim(values, first, block, 0).reshape(
            block, band_dev, HEADS, HEAD_DIM
        )
        id_block = lax.dynamic_slice_in_dim(key_ids, first, block, 0)
        scores = (
            jnp.einsum(
                "lbhe,pbhe->bhlp", query_heads, key_block, preferred_element_type=jnp.float32
            )
            * scale
        )
        allowed = (query_ids[:, None] == id_block[None, :])[None, None]
        masked = jnp.where(allowed, scores, -1e30)
        peak, total, accum = carry
        new_peak = jnp.maximum(peak, jnp.max(masked, axis=-1))
        expo = jnp.where(allowed, jnp.exp(masked - new_peak[..., None]), 0.0)
        factor = jnp.exp(peak - new_peak)
        total = total * factor + jnp.sum(expo, axis=-1)
        accum = accum * factor[..., None] + jnp.einsum(
            "bhlp,pbhe->bhle",
            expo.astype(jnp.bfloat16),
            value_block,
            preferred_element_type=jnp.float32,
        )
        return ((new_peak, total, accum), None)

    state, unused = lax.scan(step, state, jnp.arange(count // block, dtype=jnp.int32))
    return state


def empty_state(band_dev, loc_dev):
    return (
        jnp.full((band_dev, HEADS, loc_dev), -1e30, jnp.float32),
        jnp.zeros((band_dev, HEADS, loc_dev), jnp.float32),
        jnp.zeros((band_dev, HEADS, loc_dev, HEAD_DIM), jnp.float32),
    )


def heads_result(state, width):
    peak, total, accum = state
    loc_dev = total.shape[2]
    band_dev = total.shape[0]
    return (
        (accum / total[..., None])
        .transpose(2, 0, 1, 3)
        .reshape(loc_dev, band_dev, width)
        .astype(jnp.bfloat16)
    )


def split_qkv(normed, spatial_qkv, loc_dev, band_dev, width):
    packed = jnp.dot(
        normed.reshape(-1, width), spatial_qkv, preferred_element_type=jnp.float32
    ).astype(jnp.bfloat16)
    packed = packed.reshape(loc_dev, band_dev, 3, width)
    return (packed[:, :, 0], packed[:, :, 1], packed[:, :, 2])


def channel_mix(query, keys, values):
    scale = HEAD_DIM ** (-0.5)
    rows, band_query, width = query.shape
    band_keys = keys.shape[1]
    query_heads = query.reshape(rows, band_query, HEADS, HEAD_DIM)
    key_heads = keys.reshape(rows, band_keys, HEADS, HEAD_DIM)
    value_heads = values.reshape(rows, band_keys, HEADS, HEAD_DIM)
    scores = (
        jnp.einsum("rbhe,rche->rhbc", query_heads, key_heads, preferred_element_type=jnp.float32)
        * scale
    )
    peak = jnp.max(scores, axis=-1, keepdims=True)
    expo = jnp.exp(scores - peak)
    total = jnp.sum(expo, axis=-1)
    summed = jnp.einsum(
        "rhbc,rche->rbhe",
        expo.astype(jnp.bfloat16),
        value_heads,
        preferred_element_type=jnp.float32,
    )
    return (
        (summed / jnp.transpose(total, (0, 2, 1))[..., None])
        .astype(jnp.bfloat16)
        .reshape(rows, band_query, width)
    )


def channel_projections(mid, channel_qkv):
    rows, band_count, width = mid.shape
    normed = norm_rows(mid.astype(jnp.float32)).astype(jnp.bfloat16).reshape(-1, width)
    packed = jnp.dot(normed, channel_qkv, preferred_element_type=jnp.float32).astype(jnp.bfloat16)
    packed = packed.reshape(rows, band_count, 3, width)
    return (packed[:, :, 0], packed[:, :, 1], packed[:, :, 2])


def finish(mid, cattn, channel_out, up_weight, down_weight):
    rows, band_count, width = mid.shape
    after = mid.astype(jnp.float32).reshape(-1, width) + jnp.dot(
        cattn.reshape(-1, width), channel_out, preferred_element_type=jnp.float32
    )
    normed = norm_rows(after).astype(jnp.bfloat16)
    hidden = jax.nn.gelu(
        jnp.dot(normed, up_weight, preferred_element_type=jnp.float32), approximate=True
    ).astype(jnp.bfloat16)
    joined = after + jnp.dot(hidden, down_weight, preferred_element_type=jnp.float32)
    return joined.astype(jnp.bfloat16).reshape(rows, band_count, width)


def body(
    tokens,
    band_index,
    band_table,
    window_ids,
    spatial_qkv,
    spatial_out,
    channel_qkv,
    channel_out,
    up_weight,
    down_weight,
):
    loc_dev, band_dev, width = tokens.shape
    band_first = lax.axis_index("band") * band_dev
    mine = lax.dynamic_slice_in_dim(band_index, band_first, band_dev)
    onehot = (mine[:, None] == jnp.arange(band_table.shape[0], dtype=jnp.int32)[None, :]).astype(
        jnp.float32
    )
    embed = jnp.dot(onehot, band_table, precision=lax.Precision.HIGHEST)
    start = tokens.astype(jnp.float32) + embed[None]
    normed = norm_rows(start).astype(jnp.bfloat16)
    my_ids = lax.dynamic_slice_in_dim(window_ids, lax.axis_index("loc") * loc_dev, loc_dev)
    initial = empty_state(band_dev, loc_dev)
    query, keys, values = split_qkv(normed, spatial_qkv, loc_dev, band_dev, width)
    state = attend(
        initial,
        query,
        my_ids,
        lax.all_gather(keys, "loc", axis=0, tiled=True),
        lax.all_gather(values, "loc", axis=0, tiled=True),
        window_ids,
    )
    sattn = heads_result(state, width).reshape(-1, width)
    mid = (
        start.reshape(-1, width) + jnp.dot(sattn, spatial_out, preferred_element_type=jnp.float32)
    ).astype(jnp.bfloat16)
    mid = mid.reshape(loc_dev, band_dev, width)
    cquery, ckeys, cvalues = channel_projections(mid, channel_qkv)
    all_keys, all_values = (
        lax.all_gather(ckeys, "band", axis=1, tiled=True),
        lax.all_gather(cvalues, "band", axis=1, tiled=True),
    )
    cattn = channel_mix(cquery, all_keys, all_values)
    return finish(mid, cattn, channel_out, up_weight, down_weight)


def solution(mesh):
    placed = (P("loc", "band", None), P(), P(), P(), P(), P(), P(), P(), P(), P())
    return jax.shard_map(
        body, mesh=mesh, in_specs=placed, out_specs=P("loc", "band", None), check_vma=False
    )
```

profile of v0, /device:TPU:28, one launch (start us, length us, event | category | flops | bytes accessed | tf_op | source)
XLA Modules:
  0.0 1054.5 jit_solution(17593564571710563934)
XLA Ops:
  18.5 4.5 convolution_convert_fusion.1
  23.0 4.5 reshape.120
  27.6 4.4 fusion.52
  41.6 82.5 %all-gather.11.cloned.1.call-done = bf16[4096,2,1,768]{3,1,2,0:T(2,128)(2,1)} async-done(((bf16[256,2,1,768]{3,1,2,0:T(2,128)(2,1)}), bf16[4096,2,1,768]{3,1,2,0:T(2,128)(2,1)}) %all-gather.11.cloned.1.call-update) | async-done | bytes 12582928 | tf_op jit(solution)/shard_map/all_gather | solution.py:162
  124.1 90.7 %all-gather.9.cloned.1.call-done = bf16[4096,2,1,768]{3,1,2,0:T(2,128)(2,1)} async-done(((bf16[256,2,1,768]{3,1,2,0:T(2,128)(2,1)}), bf16[4096,2,1,768]{3,1,2,0:T(2,128)(2,1)}) %all-gather.9.cloned.1.call-update) | async-done | bytes 12582928 | tf_op jit(solution)/shard_map/all_gather | solution.py:161
  214.8 204.5 %while.15 = (s32[]{:T(128)}, f32[2,12,256]{2,1,0:T(8,128)S(1)}, f32[2,12,256]{2,1,0:T(8,128)S(1)}, f32[2,12,256,64]{2,3,1,0:T(8,128)}, s32[256]{0:T(256)S(1)}, /...) while((s32[]{:T(128)}, f32[2,12,256]{2,1,0:T(8,128)S(1)}, ...), condition=%wide.region_5.6_spmd.clone, body=%wide.region_2.5_spmd.clone.sunk | while | flops 847542272 | bytes 77208880 | solution.py:53
  217.0 5.2 constant_dynamic-slice_fusion.3
  222.2 3.6 copy.101
  242.6 5.2 constant_dynamic-slice_fusion.3
  247.8 3.6 copy.101
  268.1 5.2 constant_dynamic-slice_fusion.3
  273.4 3.6 copy.101
  293.7 5.2 constant_dynamic-slice_fusion.3
  298.9 3.6 copy.101
  319.2 5.2 constant_dynamic-slice_fusion.3
  324.5 3.6 copy.101
  344.8 5.2 constant_dynamic-slice_fusion.3
  370.4 5.2 constant_dynamic-slice_fusion.3
  395.9 5.2 constant_dynamic-slice_fusion.3
  432.4 4.5 reshape.121
  437.0 5.0 fusion.51
  448.1 240.9 %all-gather.13.cloned.1.call-done = bf16[256,16,1,768]{3,2,1,0:T(2,128)(2,1)} async-done(((bf16[256,2,1,768]{3,2,1,0:T(2,128)(2,1)}), bf16[256,16,1,768]{3,2,1,0:T(2,128)(2,1)}) %all-gather.13.cloned.1.call-update) | async-done | bytes 6291472 | tf_op jit(solution)/shard_map/all_gather | solution.py:173
  688.9 29.0 %copy.83 = bf16[256,16,1,768]{0,3,1,2:T(8,128)(2,1)} copy(bf16[256,16,1,768]{3,2,1,0:T(2,128)(2,1)} %all-gather.13.cloned.1.call-done) | data formatting | bytes 12582912 | tf_op jit(solution)/shard_map/all_gather | solution.py:173
  718.0 18.5 %copy.88 = bf16[256,16,12,64]{3,1,2,0:T(8,128)(2,1)} copy(bf16[256,16,12,64]{0,3,2,1:T(8,128)(2,1)} %bitcast.66) | data formatting | bytes 12582912 | tf_op jit(solution)/shard_map/reshape | solution.py:91
  736.5 201.9 %all-gather.15.cloned.1.call-done = bf16[256,16,1,768]{3,2,1,0:T(2,128)(2,1)} async-done(((bf16[256,2,1,768]{3,2,1,0:T(2,128)(2,1)}), bf16[256,16,1,768]{3,2,1,0:T(2,128)(2,1)}) %all-gather.15.cloned.1.call-update) | async-done | bytes 6291472 | tf_op jit(solution)/shard_map/all_gather | solution.py:172
  938.4 29.0 %copy.85 = bf16[256,16,1,768]{0,3,1,2:T(8,128)(2,1)} copy(bf16[256,16,1,768]{3,2,1,0:T(2,128)(2,1)} %all-gather.15.cloned.1.call-done) | data formatting | bytes 12582912 | tf_op jit(solution)/shard_map/all_gather | solution.py:172
  967.4 18.6 %copy.87 = bf16[256,16,12,64]{3,1,2,0:T(8,128)(2,1)} copy(bf16[256,16,12,64]{0,3,2,1:T(8,128)(2,1)} %bitcast.67) | data formatting | bytes 12582912 | tf_op jit(solution)/shard_map/reshape | solution.py:90
  985.9 11.5 %multiply_reduce_fusion = (f32[256,12,2]{2,1,0:T(8,128)}, f32[256,12,2,16]{3,2,1,0:T(2,128)S(1)}) fusion(bf16[256,2,12,64]{3,1,2,0:T(2,128)(2,1)} %copy.86, bf16[256,16,12,64]{3,1,2,0:T(8,128)(2,1)} %copy.87), kind=kOutput, calls=%fused_computation.32 | convolution fusion | flops 12773376 | bytes 7495680 | tf_op jit(solution)/shard_map/rbhe,rche->rhbc/dot_general | solution.py:93
  997.4 9.8 fusion.50
  1007.2 9.1 fusion.28
  1016.3 5.6 copy.89
  1033.7 11.0 %add_convert_fusion = bf16[512,768]{1,0:T(8,128)(2,1)} fusion(f32[512,768]{1,0:T(8,128)} %copy-done.11, bf16[3072,768]{1,0:T(8,128)(2,1)} %param.21, bf16[768,3072]{1,0:T(8,128)(2,1)} %param.20, f32[512]{0:T(512)S(1)} %add_rsqrt_fusion.1, f32[512]{0:T(512)S(1)} %broadcast_multiply_fusion.1), kind=kOutput, calls=%fused_computation.42 | convolution fusion | flops 4847960064 | bytes 11800576 | tf_op jit(solution)/shard_map/dot_general | solution.py:129
  (199 shorter events, 193.7 us)
Async XLA Ops:
  6.5 11.9 %copy-start = (bf16[768,2304]{1,0:T(8,128)(2,1)S(1)}, bf16[768,2304]{1,0:T(8,128)(2,1)}, u32[]{:S(2)}) copy-start(bf16[768,2304]{1,0:T(8,128)(2,1)} %param.16) | copy-start | bytes 10616836
  6.5 117.6 %all-gather.11.cloned.1.call-start = ((), (), s32[]{:S(2)}) async-start(), calls=%async_computation.1 | async-start | bytes 13369344 | tf_op jit(solution)/shard_map/all_gather | solution.py:162
  6.5 6.7 copy-start.4
  32.0 1.8 copy-start.8
  33.7 1.9 copy-start.5
  33.7 181.1 %all-gather.9.cloned.1.call-start = ((), (), s32[]{:S(2)}) async-start(), calls=%async_computation | async-start | bytes 13369344 | tf_op jit(solution)/shard_map/all_gather | solution.py:161
  35.5 2.4 copy-start.6
  35.5 653.4 %all-gather.13.cloned.1.call-start = ((), (), s32[]{:S(2)}) async-start(), calls=%async_computation.2 | async-start | bytes 14155776 | tf_op jit(solution)/shard_map/all_gather | solution.py:173
  232.6 3.1 copy-start.2
  232.6 3.1 copy-start.9
  239.3 1.1 copy-start.10
  258.2 3.1 copy-start.2
  258.2 3.1 copy-start.9
  283.7 3.1 copy-start.2
  283.8 3.1 copy-start.9
  309.3 3.1 copy-start.2
  309.3 3.1 copy-start.9
  334.9 3.1 copy-start.2
  334.9 3.1 copy-start.9
  360.4 3.1 copy-start.2
  360.4 3.1 copy-start.9
  386.0 3.1 copy-start.2
  386.0 3.1 copy-start.9
  411.5 3.1 copy-start.2
  411.6 3.1 copy-start.9
  425.3 3.7 copy-start.14
  442.0 1.4 copy-start.7
  442.1 496.3 %all-gather.15.cloned.1.call-start = ((), (), s32[]{:S(2)}) async-start(), calls=%async_computation.3 | async-start | bytes 14155776 | tf_op jit(solution)/shard_map/all_gather | solution.py:172
  1016.3 5.6 copy-start.3
  1027.5 2.3 copy-start.13
  1032.2 1.2 copy-start.11
  1033.7 13.9 %copy-start.1 = (bf16[768,2304]{1,0:T(8,128)(2,1)S(1)}, bf16[768,2304]{1,0:T(8,128)(2,1)}, u32[]{:S(2)}) copy-start(bf16[768,2304]{1,0:T(8,128)(2,1)} %param.16) | copy-start | bytes 10616836
  (8 other events, 8.9 us)
Sparse Core Ops, SparseCore 0:
  33.9 90.2 all-gather.10
  126.6 88.2 all-gather.8
  442.2 246.6 all-gather.12
  690.4 247.9 all-gather.14
where the time goes:
time: 1070 us; the launch traced here: 1050 us
  waiting for transfers between devices  617 us (58%)
  local copies, waits for them, and re-layouts  272 us (25%)
  matrix products  99.6 us (9%)
  other arithmetic  46.4 us (4%)
  between operations  13.8 us (1%)
    all_gather x1, waiting for transfers between devices, body(): lax.all_gather(cvalues, 'band', axis=1, tiled=True)  241 us
    all_gather x1, waiting for transfers between devices, body(): lax.all_gather(ckeys, 'band', axis=1, tiled=True)  202 us
    all_gather x1, waiting for transfers between devices, body(): lax.all_gather(keys, 'loc', axis=0, tiled=True)  90.7 us
    all_gather x1, waiting for transfers between devices, body(): lax.all_gather(values, 'loc', axis=0, tiled=True)  82.5 us
    dynamic_slice x16, local copies, waits for them, and re-layouts, step(): lax.dynamic_slice_in_dim(values, first, block, 0)  70.3 us
    all_gather x1, local copies, waits for them, and re-layouts, body(): lax.all_gather(cvalues, 'band', axis=1, tiled=True)  29 us
    all_gather x1, local copies, waits for them, and re-layouts, body(): lax.all_gather(ckeys, 'band', axis=1, tiled=True)  29 us
    dynamic_slice x8, local copies, waits for them, and re-layouts, step(): lax.dynamic_slice_in_dim(keys, first, block, 0)  28.7 us
  transfers between devices with their start and end apart: 4, of which 4 were waited for; matrix products, arithmetic and copies ran while one was open for 6% of the time, Pallas kernels for 0%

commit v1 on v0

v1 whole, which is shorter than its diff:
```python
import functools

import jax
import jax.numpy as jnp
from jax import lax
from jax.experimental import pallas as pl
from jax.experimental.pallas import tpu as pltpu
from jax.sharding import PartitionSpec as P

BF = jnp.bfloat16
F32 = jnp.float32
MESH = pl.DeviceIdType.MESH
NT = (((1,), (1,)), ((), ()))
QSCALE = 0.125 * 1.4426950408889634


def norm_rows(values):
    centre = values - jnp.mean(values, axis=-1, keepdims=True)
    spread = jnp.mean(centre * centre, axis=-1, keepdims=True)
    return centre * lax.rsqrt(spread + 1e-05)


def place():
    band = lax.axis_index("band")
    loc = lax.axis_index("loc")
    return band // 2, band % 2, loc // 4, (loc // 2) % 2, loc % 2


def at(y, xlo, z, xhi, core):
    return {"band": y * 2 + xlo, "loc": z * 4 + xhi * 2 + core}


def spatial_kernel(
    tok_ref, tgt_ref, bi_ref, table_ref, w_hbm,
    sattn_ref, tokch_ref,
    perm, normed, xbuf, wbuf, qbuf, kbuf, vbuf, s0, s1, m0, m1, obuf,
    wsem, a_send, a_recv, f_send, c_send, c_recv, t_send, t_recv, t_local, o_send, o_recv,
):
    y, xlo, z, xhi, core = place()
    me = lax.axis_index("band")
    loc = lax.axis_index("loc")
    flip = z + 1 - 2 * (z % 2)
    opp = 3 - z

    first = 3 * (z % 2)
    wcopies = []
    for t in range(3):
        for n, pair in enumerate((first + core, first + 2)):
            cols = pl.ds(pl.multiple_of(t * 768 + pair * 128, 128), 128)
            wcopies.append(pltpu.make_async_copy(
                w_hbm.at[:, cols], wbuf.at[:, pl.ds(t * 256 + n * 128, 128)], wsem.at[2 * t + n]))
    for c in wcopies:
        c.start()

    rows = lax.broadcasted_iota(jnp.int32, (512, 512), 0)
    select = jnp.where(rows == tgt_ref[...], 1.0, 0.0).astype(BF)
    ordered = jnp.dot(select, tok_ref[...], preferred_element_type=F32)
    for b in range(2):
        part = ordered[b * 256:(b + 1) * 256]
        perm[b] = part.astype(BF).reshape(16, 16, 768)
        row = table_ref[pl.ds(bi_ref[2 * me + b], 1), :]
        nb = norm_rows(part + row).astype(BF)
        normed[2 * b] = nb[:128]
        normed[2 * b + 1] = nb[128:]

    sends = []
    slot = xhi * 4 + z
    mine = z // 2
    for b in range(2):
        for n, (w, zt) in enumerate(((mine, z), (mine, flip), (1 - mine, opp))):
            sends.append(pltpu.make_async_remote_copy(
                normed.at[2 * b + w], xbuf.at[slot], a_send.at[3 * b + n], a_recv.at[slot],
                device_id=at(y, 1 - xlo, zt, b, core), device_id_type=MESH))
    for s in (2, 0, 1, 5, 3, 4):
        sends[s].start()

    tsends = []
    for d in range(1, 8):
        to = (me + d) % 8
        for b in range(2):
            tsends.append(pltpu.make_async_remote_copy(
                perm.at[b, pl.ds(2 * to, 2)], tokch_ref.at[:, 2 * me + b],
                t_send.at[2 * d + b - 2], t_recv.at[2 * d + b - 2],
                device_id={"band": to, "loc": loc}, device_id_type=MESH))
    for c in tsends:
        c.start()
    tlocal = [pltpu.make_async_copy(
        perm.at[b, pl.ds(2 * me, 2)], tokch_ref.at[:, 2 * me + b], t_local.at[b]) for b in range(2)]
    for c in tlocal:
        c.start()

    for c in wcopies:
        c.wait()

    def project(s, shared_q):
        x = xbuf[s]
        q = jnp.dot(x, wbuf[:, 0:256], preferred_element_type=F32) * QSCALE
        qbuf[s] = q[:, :128].astype(BF)
        if shared_q:
            qbuf[16 + s] = q[:, 128:].astype(BF)
        k = jnp.dot(x, wbuf[:, 256:512], preferred_element_type=F32)
        kbuf[0, s] = k[:, :128].astype(BF)
        kbuf[1, s] = k[:, 128:].astype(BF)
        v = jnp.dot(x, wbuf[:, 512:768], preferred_element_type=F32)
        vt = v.T.astype(BF)
        for n in range(4):
            vbuf[n, s, 0:64, :] = vt[64 * n:64 * n + 64]

    ones = jnp.ones((16, 128), BF)

    def fill(s, _):
        for n in range(4):
            vbuf[n, s, 64:80, :] = ones
        return 0

    lax.fori_loop(0, 16, fill, 0)

    def arrival(s):
        return pltpu.make_async_remote_copy(
            xbuf.at[s], xbuf.at[s], c_send.at[s], a_recv.at[s],
            device_id=at(y, xlo, z, xhi, 1 - core), device_id_type=MESH)

    def to_partner(s):
        return pltpu.make_async_remote_copy(
            xbuf.at[s], xbuf.at[8 + s], c_send.at[s], c_recv.at[s],
            device_id=at(y, xlo, z, xhi, 1 - core), device_id_type=MESH)

    def forward(s, n):
        return pltpu.make_async_remote_copy(
            xbuf.at[s], xbuf.at[s], f_send.at[n], a_recv.at[s],
            device_id=at(y, xlo, flip, xhi, core), device_id_type=MESH)

    for n in range(2):
        s = n * 4 + opp
        arrival(s).wait_recv()
        forward(s, n).start()
        to_partner(s).start()

    for zs in (z, flip, 3 - flip):
        for n in range(2):
            s = n * 4 + zs
            arrival(s).wait_recv()
            to_partner(s).start()

    def project_own(s, _):
        project(s, True)
        return 0

    lax.fori_loop(0, 8, project_own, 0)

    def project_other(s, _):
        to_partner(s).wait_recv()
        project(8 + s, False)
        return 0

    lax.fori_loop(0, 8, project_other, 0)

    lane = lax.broadcasted_iota(jnp.int32, (256, 128), 1)

    def scores(u, h, sref, mref):
        kv = u // 8
        q = qbuf[pl.ds(2 * u, 2)].reshape(256, 128)
        q = jnp.where((lane < 64) == (h == 0), q, jnp.zeros_like(q))
        peak = None
        for c in range(8):
            keys = kbuf[kv, pl.ds(2 * c, 2)].reshape(256, 128)
            st = lax.dot_general(keys, q, NT, preferred_element_type=F32)
            sref[pl.ds(c * 256, 256), :] = st
            top = jnp.max(st.reshape(32, 8, 256), axis=0)
            peak = top if peak is None else jnp.maximum(peak, top)
        mref[...] = jnp.broadcast_to(jnp.max(peak, axis=0, keepdims=True), (8, 256))

    def mix(u, h, sref, mref):
        kv = u // 8
        peak = mref[0:1, :]
        acc = None
        for c in range(8):
            p = jnp.exp2(sref[pl.ds(c * 256, 256), :] - peak).astype(BF)
            for n in range(2):
                part = jnp.dot(vbuf[kv * 2 + h, 2 * c + n], p[128 * n:128 * n + 128],
                               preferred_element_type=F32)
                acc = part if acc is None else acc + part
        return acc[:64] / acc[64:65]

    w = z // 2
    band = 2 * (y * 2 + 1 - xlo) + xhi

    def message(i, jj):
        s = i % 16
        src_core = (core + s // 8) % 2
        xs = (s % 8) // 4
        zs = s % 4
        pair = first + jnp.where(i < 16, core, 2)
        to_band = w * 4 + jj
        to_loc = zs * 4 + xs * 2 + src_core
        src = obuf.at[pl.ds(8 * i + 2 * jj, 2)]
        dst = sattn_ref.at[:, band, :, pl.ds(pl.multiple_of(pair * 128, 128), 128)]
        is_self = jnp.logical_and(to_band == me, to_loc == loc)
        remote = pltpu.make_async_remote_copy(
            src, dst, o_send, o_recv, device_id={"band": to_band, "loc": to_loc},
            device_id_type=MESH)
        return is_self, remote, pltpu.make_async_copy(src, dst, o_recv)

    def send_out(i):
        def one(jj, _):
            is_self, remote, local = message(i, jj)

            @pl.when(is_self)
            def _():
                local.start()

            @pl.when(jnp.logical_not(is_self))
            def _():
                remote.start()

            return 0

        lax.fori_loop(0, 4, one, 0)

    scores(0, 0, s0, m0)

    def unit(u, _):
        @pl.when(u > 0)
        def _():
            send_out(2 * u - 2)
            send_out(2 * u - 1)

        scores(u, 1, s1, m1)
        a = mix(u, 0, s0, m0)
        scores(jnp.minimum(u + 1, 11), 0, s0, m0)
        b = mix(u, 1, s1, m1)
        o = jnp.concatenate([a, b], axis=0).T.astype(BF)
        obuf[pl.ds(16 * u, 16)] = o.reshape(16, 16, 128)
        return 0

    lax.fori_loop(0, 12, unit, 0)
    send_out(22)
    send_out(23)

    for c in sends:
        c.wait_send()
    for n in range(2):
        forward(n * 4 + opp, n).wait_send()

    def core_done(s, _):
        to_partner(s).wait_send()
        return 0

    lax.fori_loop(0, 8, core_done, 0)
    for c in tsends:
        c.wait_send()
        c.wait_recv()
    for c in tlocal:
        c.wait()

    stays = me // 4 == w

    @pl.when(stays)
    def _():
        pltpu.make_async_copy(obuf.at[pl.ds(0, 188)], obuf.at[pl.ds(0, 188)], o_send).wait()

    @pl.when(jnp.logical_not(stays))
    def _():
        pltpu.make_async_copy(obuf, obuf, o_send).wait()

    pltpu.make_async_copy(sattn_ref, sattn_ref, o_recv).wait()


def spatial(tokens, tgt, band_index, table, spatial_qkv):
    vmem = pl.BlockSpec(memory_space=pltpu.VMEM)
    hbm = pl.BlockSpec(memory_space=pl.ANY)
    dma = pltpu.SemaphoreType.DMA
    return pl.pallas_call(
        spatial_kernel,
        out_shape=[jax.ShapeDtypeStruct((2, 16, 16, 768), BF)] * 2,
        in_specs=[vmem, vmem, pl.BlockSpec(memory_space=pltpu.SMEM), vmem, hbm],
        out_specs=[hbm, hbm],
        scratch_shapes=[
            pltpu.VMEM((2, 16, 16, 768), BF),
            pltpu.VMEM((4, 128, 768), BF),
            pltpu.VMEM((16, 128, 768), BF),
            pltpu.VMEM((768, 768), BF),
            pltpu.VMEM((24, 128, 128), BF),
            pltpu.VMEM((2, 16, 128, 128), BF),
            pltpu.VMEM((4, 16, 80, 128), BF),
            pltpu.VMEM((2048, 256), F32),
            pltpu.VMEM((2048, 256), F32),
            pltpu.VMEM((8, 256), F32),
            pltpu.VMEM((8, 256), F32),
            pltpu.VMEM((192, 16, 128), BF),
            dma((6,)), dma((6,)), dma((8,)), dma((2,)), dma((8,)), dma((8,)),
            dma((14,)), dma((14,)), dma((2,)), dma, dma,
        ],
        compiler_params=pltpu.CompilerParams(
            has_side_effects=True, vmem_limit_bytes=60 << 20),
        name="spatial",
    )(tokens, tgt, band_index, table, spatial_qkv)


def channel_kernel(
    sattn_ref, tokch_ref, bi_ref, table_ref, tgt_ref, wo_h, wc_h, wco_h, wu_h, wd_h,
    out_ref,
    wo, wc, wco, wu, wd, sa, tk, jbuf, outp,
    cat, hid, wsem, isem, j_send, j_recv, j_local,
):
    me = lax.axis_index("band")
    loc = lax.axis_index("loc")
    icopies = [pltpu.make_async_copy(sattn_ref, sa, isem.at[0]),
               pltpu.make_async_copy(tokch_ref, tk, isem.at[1])]
    for c in icopies:
        c.start()
    wcopies = [pltpu.make_async_copy(src, dst, wsem.at[n]) for n, (src, dst) in enumerate(
        ((wo_h, wo), (wc_h, wc), (wco_h, wco), (wu_h, wu), (wd_h, wd)))]
    for c in wcopies:
        c.start()
    barrier = pltpu.get_barrier_semaphore()
    for d in range(1, 8):
        pl.semaphore_signal(barrier, inc=1, device_id={"band": (me + d) % 8, "loc": loc},
                            device_id_type=MESH)
    pl.semaphore_wait(barrier, 7)
    for c in icopies:
        c.wait()
    for c in wcopies:
        c.wait()

    embed = jnp.concatenate([table_ref[pl.ds(bi_ref[n], 1), :] for n in range(16)], axis=0)
    rowi = lax.broadcasted_iota(jnp.int32, (256, 256), 0)
    coli = lax.broadcasted_iota(jnp.int32, (256, 256), 1)
    same = (rowi % 16) == (coli % 16)
    lane = lax.broadcasted_iota(jnp.int32, (256, 128), 1)

    def message(h, d):
        to = (me + d) % 8
        return pltpu.make_async_remote_copy(
            jbuf.at[h, pl.ds(2 * to, 2)], outp.at[:, 2 * me + h],
            j_send.at[8 * h + d], j_recv.at[8 * h + d],
            device_id={"band": to, "loc": loc}, device_id_type=MESH)

    def local(h):
        return pltpu.make_async_copy(
            jbuf.at[h, pl.ds(2 * me, 2)], outp.at[:, 2 * me + h], j_local.at[h])

    def half(h, _):
        start = (tk[h].astype(F32) + embed[:, None, :]).reshape(256, 768)
        mid = (start + jnp.dot(sa[h].reshape(256, 768), wo[...],
                               preferred_element_type=F32)).astype(BF)
        midf = mid.astype(F32)
        normed = norm_rows(midf).astype(BF)
        for pair in range(6):
            cols = pl.ds(pair * 128, 128)
            q = (jnp.dot(normed, wc[:, cols], preferred_element_type=F32) * QSCALE).astype(BF)
            k = jnp.dot(normed, wc[:, pl.ds(768 + pair * 128, 128)],
                        preferred_element_type=F32).astype(BF)
            v = jnp.dot(normed, wc[:, pl.ds(1536 + pair * 128, 128)],
                        preferred_element_type=F32).astype(BF)
            vx = jnp.concatenate([v, jnp.ones((256, 128), BF)], axis=1)
            res = []
            for n in range(2):
                qn = jnp.where((lane < 64) == (n == 0), q, jnp.zeros_like(q))
                s = lax.dot_general(qn, k, NT, preferred_element_type=F32)
                s = jnp.where(same, s, -1e30)
                p = jnp.exp2(s - jnp.max(s, axis=1, keepdims=True)).astype(BF)
                r = jnp.dot(p, vx, preferred_element_type=F32)
                res.append(r[:, :128] / r[:, 128:])
            cat[:, cols] = jnp.where(lane < 64, res[0], res[1]).astype(BF)
        after = midf + jnp.dot(cat[...], wco[...], preferred_element_type=F32)
        normed = norm_rows(after).astype(BF)
        for c in range(4):
            cols = pl.ds(c * 768, 768)
            up = jnp.dot(normed, wu[:, cols], preferred_element_type=F32)
            hid[:, cols] = jax.nn.gelu(up, approximate=True).astype(BF)
        joined = after + jnp.dot(hid[...], wd[...], preferred_element_type=F32)
        jbuf[h] = joined.astype(BF).reshape(16, 16, 768)
        for d in range(1, 8):
            message(h, d).start()
        local(h).start()
        return 0

    lax.fori_loop(0, 2, half, 0)
    for h in range(2):
        local(h).wait()
        for d in range(1, 8):
            message(h, d).wait_send()
            message(h, d).wait_recv()
    cols = lax.broadcasted_iota(jnp.int32, (512, 512), 1)
    select = jnp.where(cols == tgt_ref[...], 1.0, 0.0).astype(BF)
    out_ref[...] = jnp.dot(select, outp[...].reshape(512, 768),
                           preferred_element_type=F32).astype(BF)


def channel(sattn, tokch, band_index, table, tgt, weights):
    vmem = pl.BlockSpec(memory_space=pltpu.VMEM)
    hbm = pl.BlockSpec(memory_space=pl.ANY)
    dma = pltpu.SemaphoreType.DMA
    return pl.pallas_call(
        channel_kernel,
        out_shape=jax.ShapeDtypeStruct((512, 768), BF),
        in_specs=[hbm, hbm, pl.BlockSpec(memory_space=pltpu.SMEM), vmem, vmem] + [hbm] * 5,
        out_specs=vmem,
        scratch_shapes=[pltpu.VMEM(w.shape, BF) for w in weights] + [
            pltpu.VMEM((2, 16, 16, 768), BF),
            pltpu.VMEM((2, 16, 16, 768), BF),
            pltpu.VMEM((2, 16, 16, 768), BF),
            pltpu.VMEM((2, 16, 16, 768), BF),
            pltpu.VMEM((256, 768), BF),
            pltpu.VMEM((256, 3072), BF),
            dma((5,)), dma((2,)), dma((16,)), dma((16,)), dma((2,)),
        ],
        compiler_params=pltpu.CompilerParams(
            has_side_effects=True, vmem_limit_bytes=60 << 20, collective_id=1),
        name="channel",
    )(sattn, tokch, band_index, table, tgt, *weights)


def body(
    tokens, band_index, band_table, window_ids, spatial_qkv, spatial_out,
    channel_qkv, channel_out, up_weight, down_weight,
):
    loc_dev = tokens.shape[0]
    ids = lax.dynamic_slice_in_dim(window_ids, lax.axis_index("loc") * loc_dev, loc_dev)
    earlier = jnp.arange(loc_dev)[None, :] < jnp.arange(loc_dev)[:, None]
    rank = jnp.sum(jnp.where((ids[:, None] == ids[None, :]) & earlier, 1, 0), axis=1)
    pos = (ids * 128 + rank).astype(jnp.int32)
    tgt = pos[:, None] + jnp.array([[0, 256]], jnp.int32)
    sattn, tokch = spatial(
        tokens.reshape(512, 768), tgt.reshape(1, 512), band_index, band_table, spatial_qkv)
    out = channel(
        sattn, tokch, band_index, band_table, tgt.reshape(512, 1),
        (spatial_out, channel_qkv, channel_out, up_weight, down_weight))
    return out.reshape(tokens.shape)


def solution(mesh):
    placed = (P("loc", "band", None), P(), P(), P(), P(), P(), P(), P(), P(), P())
    return jax.shard_map(
        body, mesh=mesh, in_specs=placed, out_specs=P("loc", "band", None), check_vma=False
    )
```

time: 1070 us -> 118 us (0.11); the launches traced: 1050 us -> 116 us
  waiting for transfers between devices: 617 us -> 0 us
  local copies, waits for them, and re-layouts: 272 us -> 8.09 us
  Pallas kernels: 0 us -> 107 us
  matrix products: 99.6 us -> 0 us
  other arithmetic: 46.4 us -> 1.05 us
  between operations: 13.8 us -> 0.03 us
    all_gather x4 -> x0, waiting for transfers between devices: 616 us -> none  [the longest x1 241 us: body(): lax.all_gather(cvalues, 'band', axis=1, tiled=True)]
    dynamic_slice x41 -> x0, local copies, waits for them, and re-layouts: 111 us -> none  [the longest x16 70.3 us: step(): lax.dynamic_slice_in_dim(values, first, block, 0)]
    pallas_call x0 -> x2, Pallas kernels: none -> 107 us  [the longest x1 72.4 us: spatial(): pl.pallas_call(spatial_kernel, out_shape=[jax.ShapeDtypeStruct((2, 16, 16...]
    dot_general x24 -> x0, matrix products: 99.6 us -> none  [the longest x8 27.9 us: step(): jnp.einsum('bhlp,pbhe->bhle', expo.astype(jnp.bfloat16), value_block, pre...]
    all_gather x2 -> x0, local copies, waits for them, and re-layouts: 58 us -> none  [the longest x1 29 us: body(): lax.all_gather(cvalues, 'band', axis=1, tiled=True)]
    reshape x7 -> x2, local copies, waits for them, and re-layouts: 54.3 us -> 5.8 us  [the longest x1 2.95 us: body(): tokens.reshape(512, 768)]
    reduce_sum x13 -> x1, other arithmetic: 39.6 us -> 0.18 us  [body(): jnp.sum(jnp.where((ids[:, None] == ids[None, :]) & earlier, 1, 0), axis=1)]
    slice x6 -> x0, local copies, waits for them, and re-layouts: 17.4 us -> none  [the longest x4 10.8 us: split_qkv(): return (packed[:, :, 0], packed[:, :, 1], packed[:, :, 2])]
  transfers between devices with their start and end apart: 4 -> 0, of which waited for: 4 -> 0; matrix products, arithmetic and copies ran while one was open for 6% -> 0% of each run, Pallas kernels for 0% -> 0%
where the time goes in v1:
time: 118 us; the launch traced here: 116 us
  Pallas kernels  107 us (91%)
  local copies, waits for them, and re-layouts  8.09 us (7%)
    pallas_call x1, Pallas kernels, spatial(): pl.pallas_call(spatial_kernel, out_shape=[jax.ShapeDtypeStruct((2, 16, 16...  72.4 us
    pallas_call x1, Pallas kernels, channel(): pl.pallas_call(channel_kernel, out_shape=jax.ShapeDtypeStruct((512, 768),...  34.5 us
    reshape x1, local copies, waits for them, and re-layouts, body(): tokens.reshape(512, 768)  2.95 us
    reshape x1, local copies, waits for them, and re-layouts, body(): return out.reshape(tokens.shape)  2.85 us

profile of v1, /device:TPU:28, one launch (start us, length us, event | category | flops | bytes accessed | tf_op | source)
XLA Modules:
  0.0 116.2 jit_solution(4270122074173395093)
XLA Ops:
  0.0 0.8 dynamic_slice.3
  0.8 0.2 select_reduce_fusion
  0.9 0.8 multiply_add_fusion
  1.7 0.1 broadcast_add_fusion
  1.8 0.7 add.47.tgt_ref
  2.5 3.0 %reshape.55.tok_ref = bf16[512,768]{1,0:T(8,128)(2,1)} reshape(bf16[256,2,768]{2,1,0:T(2,128)(2,1)} %param.11) | data formatting | bytes 1572864 | tf_op jit(solution)/shard_map/reshape | solution.py:426
  5.5 72.4 %spatial.1 = (bf16[2,16,16,768]{3,2,1,0:T(8,128)(2,1)}, bf16[2,16,16,768]{3,2,1,0:T(8,128)(2,1)}) custom-call(bf16[512,768]{1,0:T(8,128)(2,1)} %reshape.55.tok_ref, s32[1,512]{1,0:T(1,128)} %add.47.tgt_ref, s32[16]{0:T(128)} %bi_ref.3, f32[16,768]{1,0:T(8,128)} %table_ref.3, bf16[768,2304]{1,0:T(8,128)(2,1)} %w_hbm.1), custom_call_target="tpu_custom_call" | custom-call | tf_op jit(solution)/shard_map/spatial/pallas_call | solution.py:273
  77.9 0.8 add.49.tgt_ref
  78.8 34.5 %channel.1 = bf16[512,768]{1,0:T(8,128)(2,1)} custom-call(bf16[2,16,16,768]{3,2,1,0:T(8,128)(2,1)} %get-tuple-element.7.sattn_ref, bf16[2,16,16,768]{3,2,1,0:T(8,128)(2,1)} %get-tuple-element.8.tokch_ref, s32[16]{0:T(128)} %bi_ref.3, f32[16,768]{1,0:T(8,128)} %table_ref.3, s32[512,1]{1,0:T(8,128)} %add.49.tgt_ref, bf16[768,768]{1,0:T(8,128)(2,1)} %wo_h.1, ...), custom_call_target="tpu_custom_call" | custom-call | tf_op jit(solution)/shard_map/channel/pallas_call | solution.py:395
  113.3 2.9 %reshape.56 = bf16[256,2,768]{2,1,0:T(2,128)(2,1)} reshape(bf16[512,768]{1,0:T(8,128)(2,1)} %channel.1) | data formatting | bytes 1572864 | tf_op jit(solution)/shard_map/reshape | solution.py:430
  (1 shorter events, 0.0 us)

commit v2 on v1

--- a/solution.py
+++ b/solution.py
@@ -30,11 +30,13 @@
     return {"band": y * 2 + xlo, "loc": z * 4 + xhi * 2 + core}
 
 
-def spatial_kernel(
-    tok_ref, tgt_ref, bi_ref, table_ref, w_hbm,
-    sattn_ref, tokch_ref,
+def layer_kernel(
+    tok_ref, tgtr_ref, tgtc_ref, bi_ref, table_ref, w_hbm, wo_h, wc_h, wco_h, wu_h, wd_h,
+    out_ref,
     perm, normed, xbuf, wbuf, qbuf, kbuf, vbuf, s0, s1, m0, m1, obuf,
+    wo, wc, wco, wu, wd, sattn_ref, tokch_ref, jbuf, outp, cat, qc, kc, vc, hid,
     wsem, a_send, a_recv, f_send, c_send, c_recv, t_send, t_recv, t_local, o_send, o_recv,
+    lsem, j_send, j_recv, j_local,
 ):
     y, xlo, z, xhi, core = place()
     me = lax.axis_index("band")
@@ -51,9 +53,13 @@
                 w_hbm.at[:, cols], wbuf.at[:, pl.ds(t * 256 + n * 128, 128)], wsem.at[2 * t + n]))
     for c in wcopies:
         c.start()
+    lcopies = [pltpu.make_async_copy(src, dst, lsem.at[n]) for n, (src, dst) in enumerate(
+        ((wo_h, wo), (wc_h, wc), (wco_h, wco), (wu_h, wu), (wd_h, wd)))]
+    for c in lcopies:
+        c.start()
 
     rows = lax.broadcasted_iota(jnp.int32, (512, 512), 0)
-    select = jnp.where(rows == tgt_ref[...], 1.0, 0.0).astype(BF)
+    select = jnp.where(rows == tgtr_ref[...], 1.0, 0.0).astype(BF)
     ordered = jnp.dot(select, tok_ref[...], preferred_element_type=F32)
     for b in range(2):
         part = ordered[b * 256:(b + 1) * 256]
@@ -71,7 +77,7 @@
             sends.append(pltpu.make_async_remote_copy(
                 normed.at[2 * b + w], xbuf.at[slot], a_send.at[3 * b + n], a_recv.at[slot],
                 device_id=at(y, 1 - xlo, zt, b, core), device_id_type=MESH))
-    for s in (2, 0, 1, 5, 3, 4):
+    for s in (1, 4, 2, 5, 0, 3):
         sends[s].start()
 
     tsends = []
@@ -130,30 +136,33 @@
             xbuf.at[s], xbuf.at[s], f_send.at[n], a_recv.at[s],
             device_id=at(y, xlo, flip, xhi, core), device_id_type=MESH)
 
-    for n in range(2):
-        s = n * 4 + opp
-        arrival(s).wait_recv()
-        forward(s, n).start()
-        to_partner(s).start()
-
-    for zs in (z, flip, 3 - flip):
-        for n in range(2):
-            s = n * 4 + zs
+    def source(t):
+        r = t // 2
+        zs = jnp.where(r == 0, flip, jnp.where(r == 1, opp, jnp.where(r == 2, z, 3 - flip)))
+        return (t % 2) * 4 + zs
+
+    def arrive(t, _):
+        @pl.when(t < 8)
+        def _():
+            s = source(t)
             arrival(s).wait_recv()
             to_partner(s).start()
 
-    def project_own(s, _):
-        project(s, True)
+            @pl.when(t // 2 == 1)
+            def _():
+                forward(s, t % 2).start()
+
+            project(s, True)
+
+        @pl.when(t >= 2)
+        def _():
+            s = source(t - 2)
+            to_partner(s).wait_recv()
+            project(8 + s, False)
+
         return 0
 
-    lax.fori_loop(0, 8, project_own, 0)
-
-    def project_other(s, _):
-        to_partner(s).wait_recv()
-        project(8 + s, False)
-        return 0
-
-    lax.fori_loop(0, 8, project_other, 0)
+    lax.fori_loop(0, 10, arrive, 0)
 
     lane = lax.broadcasted_iota(jnp.int32, (256, 128), 1)
 
@@ -185,37 +194,39 @@
     w = z // 2
     band = 2 * (y * 2 + 1 - xlo) + xhi
 
-    def message(i, jj):
+    def send_out(i):
         s = i % 16
         src_core = (core + s // 8) % 2
         xs = (s % 8) // 4
         zs = s % 4
         pair = first + jnp.where(i < 16, core, 2)
-        to_band = w * 4 + jj
         to_loc = zs * 4 + xs * 2 + src_core
-        src = obuf.at[pl.ds(8 * i + 2 * jj, 2)]
-        dst = sattn_ref.at[:, band, :, pl.ds(pl.multiple_of(pair * 128, 128), 128)]
-        is_self = jnp.logical_and(to_band == me, to_loc == loc)
-        remote = pltpu.make_async_remote_copy(
-            src, dst, o_send, o_recv, device_id={"band": to_band, "loc": to_loc},
-            device_id_type=MESH)
-        return is_self, remote, pltpu.make_async_copy(src, dst, o_recv)
-
-    def send_out(i):
-        def one(jj, _):
-            is_self, remote, local = message(i, jj)
-
-            @pl.when(is_self)
-            def _():
-                local.start()
-
-            @pl.when(jnp.logical_not(is_self))
-            def _():
-                remote.start()
-
-            return 0
-
-        lax.fori_loop(0, 4, one, 0)
+        cols = pl.ds(pl.multiple_of(pair * 128, 128), 128)
+        dst = sattn_ref.at[:, band, :, cols]
+
+        def remote(jj):
+            pltpu.make_async_remote_copy(
+                obuf.at[pl.ds(8 * i + 2 * jj, 2)], dst, o_send, o_recv,
+                device_id={"band": w * 4 + jj, "loc": to_loc}, device_id_type=MESH).start()
+
+        own = jnp.logical_and(me // 4 == w, to_loc == loc)
+
+        @pl.when(own)
+        def _():
+            for jj in range(4):
+                @pl.when(w * 4 + jj == me)
+                def _():
+                    pltpu.make_async_copy(
+                        obuf.at[pl.ds(8 * i + 2 * jj, 2)], dst, o_recv).start()
+
+                @pl.when(w * 4 + jj != me)
+                def _():
+                    remote(jj)
+
+        @pl.when(jnp.logical_not(own))
+        def _():
+            for jj in range(4):
+                remote(jj)
 
     scores(0, 0, s0, m0)
 
@@ -265,71 +276,12 @@
 
     pltpu.make_async_copy(sattn_ref, sattn_ref, o_recv).wait()
 
-
-def spatial(tokens, tgt, band_index, table, spatial_qkv):
-    vmem = pl.BlockSpec(memory_space=pltpu.VMEM)
-    hbm = pl.BlockSpec(memory_space=pl.ANY)
-    dma = pltpu.SemaphoreType.DMA
-    return pl.pallas_call(
-        spatial_kernel,
-        out_shape=[jax.ShapeDtypeStruct((2, 16, 16, 768), BF)] * 2,
-        in_specs=[vmem, vmem, pl.BlockSpec(memory_space=pltpu.SMEM), vmem, hbm],
-        out_specs=[hbm, hbm],
-        scratch_shapes=[
-            pltpu.VMEM((2, 16, 16, 768), BF),
-            pltpu.VMEM((4, 128, 768), BF),
-            pltpu.VMEM((16, 128, 768), BF),
-            pltpu.VMEM((768, 768), BF),
-            pltpu.VMEM((24, 128, 128), BF),
-            pltpu.VMEM((2, 16, 128, 128), BF),
-            pltpu.VMEM((4, 16, 80, 128), BF),
-            pltpu.VMEM((2048, 256), F32),
-            pltpu.VMEM((2048, 256), F32),
-            pltpu.VMEM((8, 256), F32),
-            pltpu.VMEM((8, 256), F32),
-            pltpu.VMEM((192, 16, 128), BF),
-            dma((6,)), dma((6,)), dma((8,)), dma((2,)), dma((8,)), dma((8,)),
-            dma((14,)), dma((14,)), dma((2,)), dma, dma,
-        ],
-        compiler_params=pltpu.CompilerParams(
-            has_side_effects=True, vmem_limit_bytes=60 << 20),
-        name="spatial",
-    )(tokens, tgt, band_index, table, spatial_qkv)
-
-
-def channel_kernel(
-    sattn_ref, tokch_ref, bi_ref, table_ref, tgt_ref, wo_h, wc_h, wco_h, wu_h, wd_h,
-    out_ref,
-    wo, wc, wco, wu, wd, sa, tk, jbuf, outp,
-    cat, hid, wsem, isem, j_send, j_recv, j_local,
-):
-    me = lax.axis_index("band")
-    loc = lax.axis_index("loc")
-    icopies = [pltpu.make_async_copy(sattn_ref, sa, isem.at[0]),
-               pltpu.make_async_copy(tokch_ref, tk, isem.at[1])]
-    for c in icopies:
-        c.start()
-    wcopies = [pltpu.make_async_copy(src, dst, wsem.at[n]) for n, (src, dst) in enumerate(
-        ((wo_h, wo), (wc_h, wc), (wco_h, wco), (wu_h, wu), (wd_h, wd)))]
-    for c in wcopies:
-        c.start()
-    barrier = pltpu.get_barrier_semaphore()
-    for d in range(1, 8):
-        pl.semaphore_signal(barrier, inc=1, device_id={"band": (me + d) % 8, "loc": loc},
-                            device_id_type=MESH)
-    pl.semaphore_wait(barrier, 7)
-    for c in icopies:
-        c.wait()
-    for c in wcopies:
-        c.wait()
-
     embed = jnp.concatenate([table_ref[pl.ds(bi_ref[n], 1), :] for n in range(16)], axis=0)
     rowi = lax.broadcasted_iota(jnp.int32, (256, 256), 0)
     coli = lax.broadcasted_iota(jnp.int32, (256, 256), 1)
     same = (rowi % 16) == (coli % 16)
-    lane = lax.broadcasted_iota(jnp.int32, (256, 128), 1)
-
-    def message(h, d):
+
+    def home(h, d):
         to = (me + d) % 8
         return pltpu.make_async_remote_copy(
             jbuf.at[h, pl.ds(2 * to, 2)], outp.at[:, 2 * me + h],
@@ -341,19 +293,19 @@
             jbuf.at[h, pl.ds(2 * me, 2)], outp.at[:, 2 * me + h], j_local.at[h])
 
     def half(h, _):
-        start = (tk[h].astype(F32) + embed[:, None, :]).reshape(256, 768)
-        mid = (start + jnp.dot(sa[h].reshape(256, 768), wo[...],
+        start = (tokch_ref[h].astype(F32) + embed[:, None, :]).reshape(256, 768)
+        mid = (start + jnp.dot(sattn_ref[h].reshape(256, 768), wo[...],
                                preferred_element_type=F32)).astype(BF)
         midf = mid.astype(F32)
         normed = norm_rows(midf).astype(BF)
+        qc[...] = (jnp.dot(normed, wc[:, 0:768], preferred_element_type=F32) * QSCALE).astype(BF)
+        kc[...] = jnp.dot(normed, wc[:, 768:1536], preferred_element_type=F32).astype(BF)
+        vc[...] = jnp.dot(normed, wc[:, 1536:2304], preferred_element_type=F32).astype(BF)
         for pair in range(6):
             cols = pl.ds(pair * 128, 128)
-            q = (jnp.dot(normed, wc[:, cols], preferred_element_type=F32) * QSCALE).astype(BF)
-            k = jnp.dot(normed, wc[:, pl.ds(768 + pair * 128, 128)],
-                        preferred_element_type=F32).astype(BF)
-            v = jnp.dot(normed, wc[:, pl.ds(1536 + pair * 128, 128)],
-                        preferred_element_type=F32).astype(BF)
-            vx = jnp.concatenate([v, jnp.ones((256, 128), BF)], axis=1)
+            q = qc[:, cols]
+            k = kc[:, cols]
+            vx = jnp.concatenate([vc[:, cols], jnp.ones((256, 128), BF)], axis=1)
             res = []
             for n in range(2):
                 qn = jnp.where((lane < 64) == (n == 0), q, jnp.zeros_like(q))
@@ -372,44 +324,62 @@
         joined = after + jnp.dot(hid[...], wd[...], preferred_element_type=F32)
         jbuf[h] = joined.astype(BF).reshape(16, 16, 768)
         for d in range(1, 8):
-            message(h, d).start()
+            home(h, d).start()
         local(h).start()
         return 0
 
+    for c in lcopies:
+        c.wait()
     lax.fori_loop(0, 2, half, 0)
     for h in range(2):
         local(h).wait()
         for d in range(1, 8):
-            message(h, d).wait_send()
-            message(h, d).wait_recv()
+            home(h, d).wait_send()
+            home(h, d).wait_recv()
     cols = lax.broadcasted_iota(jnp.int32, (512, 512), 1)
-    select = jnp.where(cols == tgt_ref[...], 1.0, 0.0).astype(BF)
+    select = jnp.where(cols == tgtc_ref[...], 1.0, 0.0).astype(BF)
     out_ref[...] = jnp.dot(select, outp[...].reshape(512, 768),
                            preferred_element_type=F32).astype(BF)
 
 
-def channel(sattn, tokch, band_index, table, tgt, weights):
+def layer(tokens, tgt_row, tgt_col, band_index, table, spatial_qkv, weights):
     vmem = pl.BlockSpec(memory_space=pltpu.VMEM)
     hbm = pl.BlockSpec(memory_space=pl.ANY)
     dma = pltpu.SemaphoreType.DMA
+    rows = pltpu.VMEM((2, 16, 16, 768), BF)
     return pl.pallas_call(
-        channel_kernel,
+        layer_kernel,
         out_shape=jax.ShapeDtypeStruct((512, 768), BF),
-        in_specs=[hbm, hbm, pl.BlockSpec(memory_space=pltpu.SMEM), vmem, vmem] + [hbm] * 5,
+        in_specs=[vmem, vmem, vmem, pl.BlockSpec(memory_space=pltpu.SMEM), vmem] + [hbm] * 6,
         out_specs=vmem,
-        scratch_shapes=[pltpu.VMEM(w.shape, BF) for w in weights] + [
-            pltpu.VMEM((2, 16, 16, 768), BF),
-            pltpu.VMEM((2, 16, 16, 768), BF),
-            pltpu.VMEM((2, 16, 16, 768), BF),
-            pltpu.VMEM((2, 16, 16, 768), BF),
+        scratch_shapes=[
+            rows,
+            pltpu.VMEM((4, 128, 768), BF),
+            pltpu.VMEM((16, 128, 768), BF),
+            pltpu.VMEM((768, 768), BF),
+            pltpu.VMEM((24, 128, 128), BF),
+            pltpu.VMEM((2, 16, 128, 128), BF),
+            pltpu.VMEM((4, 16, 80, 128), BF),
+            pltpu.VMEM((2048, 256), F32),
+            pltpu.VMEM((2048, 256), F32),
+            pltpu.VMEM((8, 256), F32),
+            pltpu.VMEM((8, 256), F32),
+            pltpu.VMEM((192, 16, 128), BF),
+        ] + [pltpu.VMEM(w.shape, BF) for w in weights] + [
+            rows, rows, rows, rows,
+            pltpu.VMEM((256, 768), BF),
+            pltpu.VMEM((256, 768), BF),
+            pltpu.VMEM((256, 768), BF),
             pltpu.VMEM((256, 768), BF),
             pltpu.VMEM((256, 3072), BF),
-            dma((5,)), dma((2,)), dma((16,)), dma((16,)), dma((2,)),
+            dma((6,)), dma((6,)), dma((8,)), dma((2,)), dma((8,)), dma((8,)),
+            dma((14,)), dma((14,)), dma((2,)), dma, dma,
+            dma((5,)), dma((16,)), dma((16,)), dma((2,)),
         ],
         compiler_params=pltpu.CompilerParams(
-            has_side_effects=True, vmem_limit_bytes=60 << 20, collective_id=1),
-        name="channel",
-    )(sattn, tokch, band_index, table, tgt, *weights)
+            has_side_effects=True, vmem_limit_bytes=60 << 20),
+        name="layer",
+    )(tokens, tgt_row, tgt_col, band_index, table, spatial_qkv, *weights)
 
 
 def body(
@@ -422,11 +392,9 @@
     rank = jnp.sum(jnp.where((ids[:, None] == ids[None, :]) & earlier, 1, 0), axis=1)
     pos = (ids * 128 + rank).astype(jnp.int32)
     tgt = pos[:, None] + jnp.array([[0, 256]], jnp.int32)
-    sattn, tokch = spatial(
-        tokens.reshape(512, 768), tgt.reshape(1, 512), band_index, band_table, spatial_qkv)
-    out = channel(
-        sattn, tokch, band_index, band_table, tgt.reshape(512, 1),
-        (spatial_out, channel_qkv, channel_out, up_weight, down_weight))
+    out = layer(
+        tokens.reshape(512, 768), tgt.reshape(1, 512), tgt.reshape(512, 1), band_index, band_table,
+        spatial_qkv, (spatial_out, channel_qkv, channel_out, up_weight, down_weight))
     return out.reshape(tokens.shape)
 
 

time: 118 us -> 96.9 us (0.82)
  Pallas kernels: 107 us -> 86.7 us
    pallas_call x2 -> x1, Pallas kernels: 107 us -> 86.7 us  [layer(): pl.pallas_call(layer_kernel, out_shape=jax.ShapeDtypeStruct((512, 768), B...]
where the time goes in v2:
time: 96.9 us; the launch traced here: 95.9 us
  Pallas kernels  86.7 us (89%)
  local copies, waits for them, and re-layouts  8.11 us (8%)
  other arithmetic  1.05 us (1%)
    pallas_call x1, Pallas kernels, layer(): pl.pallas_call(layer_kernel, out_shape=jax.ShapeDtypeStruct((512, 768), B...  86.7 us
    reshape x1, local copies, waits for them, and re-layouts, body(): tokens.reshape(512, 768)  2.95 us
    reshape x1, local copies, waits for them, and re-layouts, body(): return out.reshape(tokens.shape)  2.85 us

profile of v2, /device:TPU:28, one launch (start us, length us, event | category | flops | bytes accessed | tf_op | source)
XLA Modules:
  0.0 95.9 jit_solution(1030937431098856015)
XLA Ops:
  0.0 0.8 dynamic_slice.3
  0.8 0.2 select_reduce_fusion
  1.0 0.8 multiply_add_fusion
  1.7 0.1 broadcast_add_fusion
  1.8 0.7 add.47.tgtr_ref
  2.6 0.8 add.49.tgtc_ref
  3.4 3.0 %reshape.55.tok_ref = bf16[512,768]{1,0:T(8,128)(2,1)} reshape(bf16[256,2,768]{2,1,0:T(2,128)(2,1)} %param.11) | data formatting | bytes 1572864 | tf_op jit(solution)/shard_map/reshape | solution.py:396
  6.3 86.7 %layer.1 = bf16[512,768]{1,0:T(8,128)(2,1)} custom-call(bf16[512,768]{1,0:T(8,128)(2,1)} %reshape.55.tok_ref, s32[1,512]{1,0:T(1,128)} %add.47.tgtr_ref, s32[512,1]{1,0:T(8,128)} %add.49.tgtc_ref, s32[16]{0:T(128)} %bi_ref.1, f32[16,768]{1,0:T(8,128)} %table_ref.1, bf16[768,2304]{1,0:T(8,128)(2,1)} %w_hbm.1, bf16[768,768]{1,0:T(8,128)(2,1)} %wo_h.1, ...), custom_call_target="tpu_custom_call" | custom-call | tf_op jit(solution)/shard_map/layer/pallas_call | solution.py:350
  93.0 2.9 %reshape.56 = bf16[256,2,768]{2,1,0:T(2,128)(2,1)} reshape(bf16[512,768]{1,0:T(8,128)(2,1)} %layer.1) | data formatting | bytes 1572864 | tf_op jit(solution)/shard_map/reshape | solution.py:398
  (1 shorter events, 0.0 us)

commit v3 on v2

--- a/solution.py
+++ b/solution.py
@@ -11,6 +11,7 @@
 F32 = jnp.float32
 MESH = pl.DeviceIdType.MESH
 NT = (((1,), (1,)), ((), ()))
+TOK = 6
 QSCALE = 0.125 * 1.4426950408889634
 
 
@@ -31,20 +32,28 @@
 
 
 def layer_kernel(
-    tok_ref, tgtr_ref, tgtc_ref, bi_ref, table_ref, w_hbm, wo_h, wc_h, wco_h, wu_h, wd_h,
+    tok_ref, ids_ref, bi_ref, table_ref, w_hbm, wo_h, wc_h, wco_h, wu_h, wd_h,
     out_ref,
     perm, normed, xbuf, wbuf, qbuf, kbuf, vbuf, s0, s1, m0, m1, obuf,
-    wo, wc, wco, wu, wd, sattn_ref, tokch_ref, jbuf, outp, cat, qc, kc, vc, hid,
-    wsem, a_send, a_recv, f_send, c_send, c_recv, t_send, t_recv, t_local, o_send, o_recv,
+    choose, rbuf, wo, wc, wco, wu, wd, sattn_ref, tokch_ref, jbuf, outp, cat, nrm, aft, qc, kc, vc, hid,
+    wsem, a_send, a_recv, f_send, c_send, c_recv, r_send, r_recv, rf_send, t_send, t_recv, t_local, o_send, o_recv,
     lsem, j_send, j_recv, j_local,
 ):
     y, xlo, z, xhi, core = place()
     me = lax.axis_index("band")
     loc = lax.axis_index("loc")
-    flip = z + 1 - 2 * (z % 2)
-    opp = 3 - z
-
-    first = 3 * (z % 2)
+
+    def pairing(odd):
+        turned = (z + 3 * odd) % 4
+        beside = turned + 1 - 2 * (turned % 2)
+        return turned, (beside + odd) % 4, (3 - turned + odd) % 4, (3 - beside + odd) % 4
+
+    turned, flip, opp, far = pairing(xlo)
+    sturned, sflip, sopp, _ = pairing(1 - xlo)
+    w = turned // 2
+    sw = sturned // 2
+
+    first = 3 * (turned % 2)
     wcopies = []
     for t in range(3):
         for n, pair in enumerate((first + core, first + 2)):
@@ -58,27 +67,57 @@
     for c in lcopies:
         c.start()
 
-    rows = lax.broadcasted_iota(jnp.int32, (512, 512), 0)
-    select = jnp.where(rows == tgtr_ref[...], 1.0, 0.0).astype(BF)
-    ordered = jnp.dot(select, tok_ref[...], preferred_element_type=F32)
+    ids = jnp.concatenate(
+        [ids_ref[pl.ds(2 * loc, 1), :], ids_ref[pl.ds(2 * loc + 1, 1), :]], axis=1)
+    down = lax.broadcasted_iota(jnp.int32, (256, 256), 0)
+    across = lax.broadcasted_iota(jnp.int32, (256, 256), 1)
+    ones_row = jnp.broadcast_to(ids.astype(F32), (8, 256)).astype(BF)
+    earlier = jnp.where(down < across, 1.0, 0.0).astype(BF)
+    before = jnp.dot(ones_row, earlier, preferred_element_type=F32)[0:1].astype(jnp.int32)
+    count = lax.broadcasted_iota(jnp.int32, (1, 256), 1) - before
+    target = jnp.where(ids == 1, 128 + before, count)
+    select = jnp.where(down == target, 1.0, 0.0).astype(BF)
+    choose[...] = select
     for b in range(2):
-        part = ordered[b * 256:(b + 1) * 256]
+        part = jnp.dot(select, tok_ref[:, b, :], preferred_element_type=F32)
         perm[b] = part.astype(BF).reshape(16, 16, 768)
         row = table_ref[pl.ds(bi_ref[2 * me + b], 1), :]
         nb = norm_rows(part + row).astype(BF)
         normed[2 * b] = nb[:128]
         normed[2 * b + 1] = nb[128:]
 
+    slot = xhi * 4 + z
+    lead = core == 0
     sends = []
-    slot = xhi * 4 + z
-    mine = z // 2
-    for b in range(2):
-        for n, (w, zt) in enumerate(((mine, z), (mine, flip), (1 - mine, opp))):
+    for n in range(2):
+        opposite = lead if n == 0 else jnp.logical_not(lead)
+        for b in range(2):
             sends.append(pltpu.make_async_remote_copy(
-                normed.at[2 * b + w], xbuf.at[slot], a_send.at[3 * b + n], a_recv.at[slot],
-                device_id=at(y, 1 - xlo, zt, b, core), device_id_type=MESH))
-    for s in (1, 4, 2, 5, 0, 3):
-        sends[s].start()
+                normed.at[2 * b + jnp.where(opposite, 1 - sw, sw)], xbuf.at[slot],
+                a_send.at[2 * n + b], a_recv.at[slot],
+                device_id=at(y, 1 - xlo, jnp.where(opposite, sopp, z), b, core),
+                device_id_type=MESH))
+
+    def relay(b):
+        return pltpu.make_async_remote_copy(
+            normed.at[2 * b + sw], rbuf.at[b], r_send.at[b], r_recv.at[b],
+            device_id=at(y, xlo, sflip, xhi, core), device_id_type=MESH)
+
+    def relayed(b):
+        return pltpu.make_async_remote_copy(
+            rbuf.at[b], xbuf.at[xhi * 4 + sflip], rf_send.at[b], a_recv.at[xhi * 4 + sflip],
+            device_id=at(y, 1 - xlo, z, b, core), device_id_type=MESH)
+
+    for c in sends[:2]:
+        c.start()
+
+    @pl.when(lead)
+    def _():
+        relay(0).start()
+        relay(1).start()
+
+    for c in sends[2:]:
+        c.start()
 
     tsends = []
     for d in range(1, 8):
@@ -88,8 +127,6 @@
                 perm.at[b, pl.ds(2 * to, 2)], tokch_ref.at[:, 2 * me + b],
                 t_send.at[2 * d + b - 2], t_recv.at[2 * d + b - 2],
                 device_id={"band": to, "loc": loc}, device_id_type=MESH))
-    for c in tsends:
-        c.start()
     tlocal = [pltpu.make_async_copy(
         perm.at[b, pl.ds(2 * me, 2)], tokch_ref.at[:, 2 * me + b], t_local.at[b]) for b in range(2)]
     for c in tlocal:
@@ -136,27 +173,41 @@
             xbuf.at[s], xbuf.at[s], f_send.at[n], a_recv.at[s],
             device_id=at(y, xlo, flip, xhi, core), device_id_type=MESH)
 
-    def source(t):
+    def source(t, zero):
         r = t // 2
-        zs = jnp.where(r == 0, flip, jnp.where(r == 1, opp, jnp.where(r == 2, z, 3 - flip)))
-        return (t % 2) * 4 + zs
+        early = jnp.where(zero == (r == 0), opp, z)
+        return (t % 2) * 4 + jnp.where(r < 2, early, jnp.where(r == 2, flip, far))
 
     def arrive(t, _):
         @pl.when(t < 8)
         def _():
-            s = source(t)
+            s = source(t, lead)
             arrival(s).wait_recv()
             to_partner(s).start()
 
-            @pl.when(t // 2 == 1)
+            @pl.when(s % 4 == opp)
             def _():
                 forward(s, t % 2).start()
 
+            @pl.when(jnp.logical_and(s % 4 == z, jnp.logical_not(lead)))
+            def _():
+                forward(s, 2 + t % 2).start()
+
+            @pl.when(jnp.logical_and(t < 2, lead))
+            def _():
+                relay(t).wait_recv()
+                relayed(t).start()
+
+            @pl.when(t == TOK)
+            def _():
+                for c in tsends:
+                    c.start()
+
             project(s, True)
 
         @pl.when(t >= 2)
         def _():
-            s = source(t - 2)
+            s = source(t - 2, jnp.logical_not(lead))
             to_partner(s).wait_recv()
             project(8 + s, False)
 
@@ -191,7 +242,6 @@
                 acc = part if acc is None else acc + part
         return acc[:64] / acc[64:65]
 
-    w = z // 2
     band = 2 * (y * 2 + 1 - xlo) + xhi
 
     def send_out(i):
@@ -252,6 +302,18 @@
         c.wait_send()
     for n in range(2):
         forward(n * 4 + opp, n).wait_send()
+
+    @pl.when(lead)
+    def _():
+        for b in range(2):
+            relay(b).wait_send()
+            relayed(b).wait_send()
+
+    @pl.when(jnp.logical_not(lead))
+    def _():
+        for n in range(2):
+            forward(n * 4 + z, 2 + n).wait_send()
+
 
     def core_done(s, _):
         to_partner(s).wait_send()
@@ -316,15 +378,21 @@
                 res.append(r[:, :128] / r[:, 128:])
             cat[:, cols] = jnp.where(lane < 64, res[0], res[1]).astype(BF)
         after = midf + jnp.dot(cat[...], wco[...], preferred_element_type=F32)
-        normed = norm_rows(after).astype(BF)
-        for c in range(4):
-            cols = pl.ds(c * 768, 768)
-            up = jnp.dot(normed, wu[:, cols], preferred_element_type=F32)
-            hid[:, cols] = jax.nn.gelu(up, approximate=True).astype(BF)
-        joined = after + jnp.dot(hid[...], wd[...], preferred_element_type=F32)
-        jbuf[h] = joined.astype(BF).reshape(16, 16, 768)
-        for d in range(1, 8):
-            home(h, d).start()
+        nrm[...] = norm_rows(after).astype(BF)
+        aft[...] = after
+        for g in range(2):
+            rows_g = pl.ds(128 * g, 128)
+            x = nrm[rows_g, :]
+            for c in range(4):
+                cols = pl.ds(c * 768, 768)
+                up = jnp.dot(x, wu[:, cols], preferred_element_type=F32)
+                hid[rows_g, cols] = jax.nn.gelu(up, approximate=True).astype(BF)
+            joined = aft[rows_g, :] + jnp.dot(hid[rows_g, :], wd[...], preferred_element_type=F32)
+            jbuf[h, pl.ds(8 * g, 8)] = joined.astype(BF).reshape(8, 16, 768)
+            for d in range(1, 8):
+                @pl.when(((me + d) % 8) // 4 == g)
+                def _():
+                    home(h, d).start()
         local(h).start()
         return 0
 
@@ -336,21 +404,21 @@
         for d in range(1, 8):
             home(h, d).wait_send()
             home(h, d).wait_recv()
-    cols = lax.broadcasted_iota(jnp.int32, (512, 512), 1)
-    select = jnp.where(cols == tgtc_ref[...], 1.0, 0.0).astype(BF)
-    out_ref[...] = jnp.dot(select, outp[...].reshape(512, 768),
-                           preferred_element_type=F32).astype(BF)
-
-
-def layer(tokens, tgt_row, tgt_col, band_index, table, spatial_qkv, weights):
+    for b in range(2):
+        out_ref[:, b, :] = lax.dot_general(
+            choose[...], outp[b].reshape(256, 768), (((0,), (0,)), ((), ())),
+            preferred_element_type=F32).astype(BF)
+
+
+def layer(tokens, window_ids, band_index, table, spatial_qkv, weights):
     vmem = pl.BlockSpec(memory_space=pltpu.VMEM)
     hbm = pl.BlockSpec(memory_space=pl.ANY)
     dma = pltpu.SemaphoreType.DMA
     rows = pltpu.VMEM((2, 16, 16, 768), BF)
     return pl.pallas_call(
         layer_kernel,
-        out_shape=jax.ShapeDtypeStruct((512, 768), BF),
-        in_specs=[vmem, vmem, vmem, pl.BlockSpec(memory_space=pltpu.SMEM), vmem] + [hbm] * 6,
+        out_shape=jax.ShapeDtypeStruct((256, 2, 768), BF),
+        in_specs=[vmem, vmem, pl.BlockSpec(memory_space=pltpu.SMEM), vmem] + [hbm] * 6,
         out_specs=vmem,
         scratch_shapes=[
             rows,
@@ -365,37 +433,35 @@
             pltpu.VMEM((8, 256), F32),
             pltpu.VMEM((8, 256), F32),
             pltpu.VMEM((192, 16, 128), BF),
+            pltpu.VMEM((256, 256), BF),
+            pltpu.VMEM((2, 128, 768), BF),
         ] + [pltpu.VMEM(w.shape, BF) for w in weights] + [
             rows, rows, rows, rows,
             pltpu.VMEM((256, 768), BF),
             pltpu.VMEM((256, 768), BF),
+            pltpu.VMEM((256, 768), F32),
+            pltpu.VMEM((256, 768), BF),
             pltpu.VMEM((256, 768), BF),
             pltpu.VMEM((256, 768), BF),
             pltpu.VMEM((256, 3072), BF),
-            dma((6,)), dma((6,)), dma((8,)), dma((2,)), dma((8,)), dma((8,)),
+            dma((6,)), dma((4,)), dma((8,)), dma((4,)), dma((8,)), dma((8,)),
+            dma((2,)), dma((2,)), dma((2,)),
             dma((14,)), dma((14,)), dma((2,)), dma, dma,
             dma((5,)), dma((16,)), dma((16,)), dma((2,)),
         ],
         compiler_params=pltpu.CompilerParams(
             has_side_effects=True, vmem_limit_bytes=60 << 20),
         name="layer",
-    )(tokens, tgt_row, tgt_col, band_index, table, spatial_qkv, *weights)
+    )(tokens, window_ids, band_index, table, spatial_qkv, *weights)
 
 
 def body(
     tokens, band_index, band_table, window_ids, spatial_qkv, spatial_out,
     channel_qkv, channel_out, up_weight, down_weight,
 ):
-    loc_dev = tokens.shape[0]
-    ids = lax.dynamic_slice_in_dim(window_ids, lax.axis_index("loc") * loc_dev, loc_dev)
-    earlier = jnp.arange(loc_dev)[None, :] < jnp.arange(loc_dev)[:, None]
-    rank = jnp.sum(jnp.where((ids[:, None] == ids[None, :]) & earlier, 1, 0), axis=1)
-    pos = (ids * 128 + rank).astype(jnp.int32)
-    tgt = pos[:, None] + jnp.array([[0, 256]], jnp.int32)
-    out = layer(
-        tokens.reshape(512, 768), tgt.reshape(1, 512), tgt.reshape(512, 1), band_index, band_table,
-        spatial_qkv, (spatial_out, channel_qkv, channel_out, up_weight, down_weight))
-    return out.reshape(tokens.shape)
+    return layer(
+        tokens, window_ids.reshape(32, 128), band_index, band_table, spatial_qkv,
+        (spatial_out, channel_qkv, channel_out, up_weight, down_weight))
 
 
 def solution(mesh):

time: 96.9 us -> 87.9 us (0.907)
  local copies, waits for them, and re-layouts: 8.11 us -> 2.55 us
  Pallas kernels: 86.7 us -> 85.1 us
  other arithmetic: 1.05 us -> 0 us
    reshape x2 -> x0, local copies, waits for them, and re-layouts: 5.8 us -> none  [the longest x1 2.95 us: body(): tokens.reshape(512, 768)]
    unnamed x0 -> x1, local copies, waits for them, and re-layouts: none -> 2.55 us
    add x2 -> x0, local copies, waits for them, and re-layouts: 1.55 us -> none  [body(): tgt = pos[:, None] + jnp.array([[0, 256]], jnp.int32)]
    pallas_call x1, Pallas kernels: 86.7 us -> 85.1 us  [layer(): pl.pallas_call(layer_kernel, out_shape=jax.ShapeDtypeStruct((256, 2, 768)...]
where the time goes in v3:
time: 87.9 us; the launch traced here: 87.7 us
  Pallas kernels  85.1 us (97%)
  local copies, waits for them, and re-layouts  2.55 us (3%)
    pallas_call x1, Pallas kernels, layer(): pl.pallas_call(layer_kernel, out_shape=jax.ShapeDtypeStruct((256, 2, 768)...  85.1 us
    unnamed x1, local copies, waits for them, and re-layouts  2.55 us

profile of v3, /device:TPU:28, one launch (start us, length us, event | category | flops | bytes accessed | tf_op | source)
XLA Modules:
  0.0 87.7 jit_solution(16320720982804416443)
XLA Ops:
  0.0 85.1 %layer.1 = bf16[256,2,768]{2,1,0:T(2,128)(2,1)} custom-call(bf16[256,2,768]{2,1,0:T(2,128)(2,1)} %tok_ref.1, s32[32,128]{1,0:T(8,128)} %bitcast.1, s32[16]{0:T(128)} %bi_ref.1, f32[16,768]{1,0:T(8,128)} %table_ref.1, bf16[768,2304]{1,0:T(8,128)(2,1)} %w_hbm.1, bf16[768,768]{1,0:T(8,128)(2,1)} %wo_h.1, bf16[768,2304]{1,0:T(8,128)(2,1)} %wc_h.1, ...), custom_call_target="tpu_custom_call" | custom-call | tf_op jit(solution)/shard_map/layer/pallas_call | solution.py:418
  85.1 2.6 %copy.12 = bf16[256,2,768]{2,1,0:T(2,128)(2,1)} copy(bf16[256,2,768]{2,1,0:T(2,128)(2,1)} %layer.1) | data formatting | bytes 1572864

commit v4 on v3

--- a/solution.py
+++ b/solution.py
@@ -33,9 +33,9 @@
 
 def layer_kernel(
     tok_ref, ids_ref, bi_ref, table_ref, w_hbm, wo_h, wc_h, wco_h, wu_h, wd_h,
-    out_ref,
+    outp, choose_ref,
     perm, normed, xbuf, wbuf, qbuf, kbuf, vbuf, s0, s1, m0, m1, obuf,
-    choose, rbuf, wo, wc, wco, wu, wd, sattn_ref, tokch_ref, jbuf, outp, cat, nrm, aft, qc, kc, vc, hid,
+    choose, rbuf, wo, wc, wco, wu, wd, sattn_ref, tokch_ref, jbuf, cat, nrm, aft, qc, kc, vc, hid,
     wsem, a_send, a_recv, f_send, c_send, c_recv, r_send, r_recv, rf_send, t_send, t_recv, t_local, o_send, o_recv,
     lsem, j_send, j_recv, j_local,
 ):
@@ -404,9 +404,13 @@
         for d in range(1, 8):
             home(h, d).wait_send()
             home(h, d).wait_recv()
+    choose_ref[...] = choose[...]
+
+
+def restore_kernel(rows_ref, choose_ref, out_ref):
     for b in range(2):
         out_ref[:, b, :] = lax.dot_general(
-            choose[...], outp[b].reshape(256, 768), (((0,), (0,)), ((), ())),
+            choose_ref[...], rows_ref[b].reshape(256, 256), (((0,), (0,)), ((), ())),
             preferred_element_type=F32).astype(BF)
 
 
@@ -415,11 +419,11 @@
     hbm = pl.BlockSpec(memory_space=pl.ANY)
     dma = pltpu.SemaphoreType.DMA
     rows = pltpu.VMEM((2, 16, 16, 768), BF)
-    return pl.pallas_call(
+    ordered, choose = pl.pallas_call(
         layer_kernel,
-        out_shape=jax.ShapeDtypeStruct((256, 2, 768), BF),
+        out_shape=[jax.ShapeDtypeStruct((2, 16, 16, 768), BF), jax.ShapeDtypeStruct((256, 256), BF)],
         in_specs=[vmem, vmem, pl.BlockSpec(memory_space=pltpu.SMEM), vmem] + [hbm] * 6,
-        out_specs=vmem,
+        out_specs=[hbm, vmem],
         scratch_shapes=[
             rows,
             pltpu.VMEM((4, 128, 768), BF),
@@ -436,7 +440,7 @@
             pltpu.VMEM((256, 256), BF),
             pltpu.VMEM((2, 128, 768), BF),
         ] + [pltpu.VMEM(w.shape, BF) for w in weights] + [
-            rows, rows, rows, rows,
+            rows, rows, rows,
             pltpu.VMEM((256, 768), BF),
             pltpu.VMEM((256, 768), BF),
             pltpu.VMEM((256, 768), F32),
@@ -453,6 +457,17 @@
             has_side_effects=True, vmem_limit_bytes=60 << 20),
         name="layer",
     )(tokens, window_ids, band_index, table, spatial_qkv, *weights)
+    return pl.pallas_call(
+        restore_kernel,
+        out_shape=jax.ShapeDtypeStruct((256, 2, 768), BF),
+        grid=(3,),
+        in_specs=[
+            pl.BlockSpec((2, 16, 16, 256), lambda i: (0, 0, 0, i)),
+            pl.BlockSpec((256, 256), lambda i: (0, 0)),
+        ],
+        out_specs=pl.BlockSpec((256, 2, 256), lambda i: (0, 0, i)),
+        name="restore",
+    )(ordered, choose)
 
 
 def body(

time: 87.9 us -> 88.3 us (level)
  Pallas kernels: 85.1 us -> 88.1 us
  local copies, waits for them, and re-layouts: 2.55 us -> 0 us
    pallas_call x1 -> x2, Pallas kernels: 85.1 us -> 88.1 us  [the longest x1 84.5 us: layer(): pl.pallas_call(layer_kernel, out_shape=[jax.ShapeDtypeStruct((2, 16, 16,...]
    unnamed x1 -> x0, local copies, waits for them, and re-layouts: 2.55 us -> none
where the time goes in v4:
time: 88.3 us; the launch traced here: 88.1 us
  Pallas kernels  88.1 us (100%)
    pallas_call x1, Pallas kernels, layer(): pl.pallas_call(layer_kernel, out_shape=[jax.ShapeDtypeStruct((2, 16, 16,...  84.5 us
    pallas_call x1, Pallas kernels, layer(): pl.pallas_call(restore_kernel, out_shape=jax.ShapeDtypeStruct((256, 2, 76...  3.61 us

profile of v4, /device:TPU:28, one launch (start us, length us, event | category | flops | bytes accessed | tf_op | source)
XLA Modules:
  0.0 88.1 jit_solution(1887672682794779183)
XLA Ops:
  0.0 84.5 %layer.1 = (bf16[2,16,16,768]{3,2,1,0:T(8,128)(2,1)}, bf16[256,256]{1,0:T(8,128)(2,1)}) custom-call(bf16[256,2,768]{2,1,0:T(2,128)(2,1)} %tok_ref.1, s32[32,128]{1,0:T(8,128)} %bitcast.1, s32[16]{0:T(128)} %bi_ref.1, f32[16,768]{1,0:T(8,128)} %table_ref.1, bf16[768,2304]{1,0:T(8,128)(2,1)} %w_hbm.1, bf16[768,768]{1,0:T(8,128)(2,1)} %wo_h.1, ...), custom_call_target="tpu_custom_call" | custom-call | tf_op jit(solution)/shard_map/layer/pallas_call | solution.py:422
  84.5 3.6 %restore.1 = bf16[256,2,768]{2,1,0:T(2,128)(2,1)} custom-call(bf16[2,16,16,768]{3,2,1,0:T(8,128)(2,1)} %get-tuple-element.7.rows_ref, bf16[256,256]{1,0:T(8,128)(2,1)} %get-tuple-element.8.choose_ref), custom_call_target="tpu_custom_call" | custom-call | tf_op jit(solution)/shard_map/restore/pallas_call | solution.py:460

commit v5 on v4

--- a/solution.py
+++ b/solution.py
@@ -410,7 +410,7 @@
 def restore_kernel(rows_ref, choose_ref, out_ref):
     for b in range(2):
         out_ref[:, b, :] = lax.dot_general(
-            choose_ref[...], rows_ref[b].reshape(256, 256), (((0,), (0,)), ((), ())),
+            choose_ref[...], rows_ref[b].reshape(256, 768), (((0,), (0,)), ((), ())),
             preferred_element_type=F32).astype(BF)
 
 
@@ -460,12 +460,8 @@
     return pl.pallas_call(
         restore_kernel,
         out_shape=jax.ShapeDtypeStruct((256, 2, 768), BF),
-        grid=(3,),
-        in_specs=[
-            pl.BlockSpec((2, 16, 16, 256), lambda i: (0, 0, 0, i)),
-            pl.BlockSpec((256, 256), lambda i: (0, 0)),
-        ],
-        out_specs=pl.BlockSpec((256, 2, 256), lambda i: (0, 0, i)),
+        in_specs=[vmem, vmem],
+        out_specs=vmem,
         name="restore",
     )(ordered, choose)
 

time: 88.3 us -> 87.2 us (0.988)
  Pallas kernels: 88.1 us -> 87.1 us
    pallas_call x1, Pallas kernels: 3.61 us -> 2.6 us  [layer(): pl.pallas_call(restore_kernel, out_shape=jax.ShapeDtypeStruct((256, 2, 76...]
where the time goes in v5:
time: 87.2 us; the launch traced here: 87.1 us
  Pallas kernels  87.1 us (100%)
    pallas_call x1, Pallas kernels, layer(): pl.pallas_call(layer_kernel, out_shape=[jax.ShapeDtypeStruct((2, 16, 16,...  84.5 us
    pallas_call x1, Pallas kernels, layer(): pl.pallas_call(restore_kernel, out_shape=jax.ShapeDtypeStruct((256, 2, 76...  2.6 us

profile of v5, /device:TPU:28, one launch (start us, length us, event | category | flops | bytes accessed | tf_op | source)
XLA Modules:
  0.0 87.1 jit_solution(9108513954223674151)
XLA Ops:
  0.0 84.5 %layer.1 = (bf16[2,16,16,768]{3,2,1,0:T(8,128)(2,1)}, bf16[256,256]{1,0:T(8,128)(2,1)}) custom-call(bf16[256,2,768]{2,1,0:T(2,128)(2,1)} %tok_ref.1, s32[32,128]{1,0:T(8,128)} %bitcast.1, s32[16]{0:T(128)} %bi_ref.1, f32[16,768]{1,0:T(8,128)} %table_ref.1, bf16[768,2304]{1,0:T(8,128)(2,1)} %w_hbm.1, bf16[768,768]{1,0:T(8,128)(2,1)} %wo_h.1, ...), custom_call_target="tpu_custom_call" | custom-call | tf_op jit(solution)/shard_map/layer/pallas_call | solution.py:422
  84.5 2.6 %restore.1 = bf16[256,2,768]{2,1,0:T(2,128)(2,1)} custom-call(bf16[2,16,16,768]{3,2,1,0:T(8,128)(2,1)} %get-tuple-element.7.rows_ref, bf16[256,256]{1,0:T(8,128)(2,1)} %get-tuple-element.8.choose_ref), custom_call_target="tpu_custom_call" | custom-call | tf_op jit(solution)/shard_map/restore/pallas_call | solution.py:460
